TPU v7x, 32 devices: a whole 2x2x4 slice. The times are simulated.
32 devices in a mesh: row: 4 (over x, core), col: 8 (over z, y).
Axes of the slice: x: 2, y: 2, z: 4, core: 2. Of those that a mesh axis runs over, the one named last changes fastest.
Arguments:
- right_sides: float32 [3, 4, 512, 64], P(None, None, 'row'), may hold values from -6 to 6
- diag_inverse: float32 [3, 4, 512, 512], replicated, as said below
- sub_blocks: float32 [3, 4, 4, 512, 512], P(None, None, None, 'row', 'col'), may hold values from -0.125 to 0.125
- block_mask: int32 [3, 4, 4], replicated, may hold values 0 or 1
- anc_values: float32 [2, 4, 512, 512], P(None, None, 'row', 'col'), may hold values from -0.09375 to 0.09375
- anc_rows: int32 [2, 4, 512], P(None, None, 'row'), may hold values from 0 to 2047, as said below
- anc_count: int32 [2, 4], replicated, may hold values from 256 to 512, as said below
- far_factor: float32 [4, 512, 32768], P(None, 'col', 'row'), may hold values from -0.1875 to 0.1875
- far_rhs: float32 [32768, 64], P(('row', 'col')), may hold values from -6 to 6
- far_solution: float32 [32768, 64], P('row'), may hold values from -4 to 4
Outputs:
- forward_solution: float32 [3, 4, 512, 64], P(None, None, 'row')
- solution: float32 [3, 4, 512, 64], P(None, None, 'row')
- far_update: float32 [32768, 64], P(('row', 'col'))
Inputs may be any that keep to these rules, and one draw needn't show every extreme that they name: `diag_inverse`: each diagonal-block inverse is lower triangular. `anc_rows`: each list holds distinct rows of the parent's window in ascending order; entries at positions anc_count or later are not used. `anc_count`: some list is full and some holds exactly 256 live entries in every draw. `block_mask`: entries on and above the block diagonal are not used.
All inputs are finite; a program needn't handle non-finite values.
Results may differ from a plain program's by a relative error of at most 0.0001.
Values sent between devices are 32-bit elements; how exact they have to be, the bound alone decides.
A program may use at most 128 MiB of HBM per device.

v0:
```python
import jax
import jax.numpy as jnp
from jax import lax
from jax.sharding import PartitionSpec as P

FULL_PRECISION = lax.Precision.HIGHEST


def strict_lower(length):
    positions = jnp.arange(length)
    return (positions[:, None] > positions[None, :]).astype(jnp.float32)


def whole_forward(right_whole, inverse, lower_blocks, weights, extra, pair_of):
    panels = right_whole.shape[1]
    solved = []
    for panel_index in range(panels):
        residual = right_whole[:, panel_index] - extra[:, panel_index]
        for earlier in range(panel_index):
            block = lower_blocks[:, pair_of[panel_index, earlier]]
            term = jnp.einsum("bij,bjk->bik", block, solved[earlier], precision=FULL_PRECISION)
            residual = residual - term * weights[:, panel_index, earlier][:, None, None]
        solved.append(
            jnp.einsum("bij,bjk->bik", inverse[:, panel_index], residual, precision=FULL_PRECISION)
        )
    return jnp.stack(solved, axis=1)


def whole_backward(forward, inverse, lower_blocks, weights, extra, pair_of):
    panels = forward.shape[1]
    solved = [None] * panels
    for panel_index in reversed(range(panels)):
        residual = forward[:, panel_index] - extra[:, panel_index]
        for later in range(panel_index + 1, panels):
            block = lower_blocks[:, pair_of[later, panel_index]]
            term = jnp.einsum("bij,bik->bjk", block, solved[later], precision=FULL_PRECISION)
            residual = residual - term * weights[:, later, panel_index][:, None, None]
        solved[panel_index] = jnp.einsum(
            "bji,bjk->bik", inverse[:, panel_index], residual, precision=FULL_PRECISION
        )
    return jnp.stack(solved, axis=1)


def place_columns(local_term, col_start, width):
    shape = local_term.shape[:-2] + (width, local_term.shape[-1])
    return lax.dynamic_update_slice_in_dim(
        jnp.zeros(shape, jnp.float32), local_term, col_start, local_term.ndim - 2
    )


def on_device(
    right_sides,
    diag_inverse,
    sub_blocks,
    block_mask,
    anc_values,
    anc_rows,
    anc_count,
    far_factor,
    far_rhs,
    far_solution,
):
    row_width = right_sides.shape[2]
    col_width = sub_blocks.shape[4]
    columns = right_sides.shape[3]
    panels = diag_inverse.shape[1]
    width = diag_inverse.shape[2]
    row_start = lax.axis_index("row") * row_width
    col_start = lax.axis_index("col") * col_width
    kept_blocks = block_mask.astype(jnp.float32) * strict_lower(panels)[None]
    anc_width = anc_rows.shape[2]
    position = lax.axis_index("row") * anc_width + jnp.arange(anc_width)
    live_rows = (position[None, None, :] < anc_count[:, :, None]).astype(jnp.float32)
    pair_list_rows = [later for later in range(panels) for earlier in range(later)]
    pair_list_cols = [earlier for later in range(panels) for earlier in range(later)]
    pair_of = {}
    for pair_index in range(len(pair_list_rows)):
        pair_of[pair_list_rows[pair_index], pair_list_cols[pair_index]] = pair_index
    pair_rows = jnp.array(pair_list_rows, dtype=jnp.int32)
    pair_cols = jnp.array(pair_list_cols, dtype=jnp.int32)
    lower_local = sub_blocks[:, pair_rows, pair_cols]
    lower_part = lax.all_gather(lower_local, "row", axis=2, tiled=True)
    lower_blocks = lax.all_gather(lower_part, "col", axis=3, tiled=True)
    right_whole = lax.all_gather(right_sides, "row", axis=2, tiled=True)
    zero_extra = jnp.zeros((2, panels, width, columns), jnp.float32)
    child_forward = whole_forward(
        right_whole[:2], diag_inverse[:2], lower_blocks[:2], kept_blocks[:2], zero_extra, pair_of
    )
    child_cols = lax.dynamic_slice_in_dim(child_forward, col_start, col_width, 2)
    updates = jnp.einsum("spaj,spjk->spak", anc_values, child_cols, precision=FULL_PRECISION)
    updates = updates * live_rows[..., None]
    spread = (
        jnp.zeros((panels * width, columns), jnp.float32)
        .at[anc_rows.reshape(-1)]
        .add(updates.reshape(-1, columns))
    )
    ancestor = lax.psum(spread, ("row", "col")).reshape(panels, width, columns)
    parent_forward = whole_forward(
        right_whole[2:],
        diag_inverse[2:],
        lower_blocks[2:],
        kept_blocks[2:],
        ancestor[None],
        pair_of,
    )
    parent_cols = lax.dynamic_slice_in_dim(parent_forward[0], col_start, col_width, 1)
    far_update = far_rhs - lax.psum_scatter(
        jnp.einsum("pjr,pjk->rk", far_factor, parent_cols, precision=FULL_PRECISION),
        "col",
        scatter_dimension=0,
        tiled=True,
    )
    far_back = jnp.einsum("pjr,rk->pjk", far_factor, far_solution, precision=FULL_PRECISION)
    far_whole = lax.psum(place_columns(far_back, col_start, width), ("row", "col"))
    parent_solution = whole_backward(
        parent_forward,
        diag_inverse[2:],
        lower_blocks[2:],
        kept_blocks[2:],
        far_whole[None],
        pair_of,
    )
    parent_flat = parent_solution[0].reshape(panels * width, columns)
    picked = parent_flat[anc_rows] * live_rows[..., None]
    child_extra = jnp.einsum("spaj,spak->spjk", anc_values, picked, precision=FULL_PRECISION)
    extra_whole = lax.psum(place_columns(child_extra, col_start, width), ("row", "col"))
    child_solution = whole_backward(
        child_forward, diag_inverse[:2], lower_blocks[:2], kept_blocks[:2], extra_whole, pair_of
    )
    forward_all = jnp.concatenate([child_forward, parent_forward], axis=0)
    solution_all = jnp.concatenate([child_solution, parent_solution], axis=0)
    forward_rows = lax.dynamic_slice_in_dim(forward_all, row_start, row_width, 2)
    solution_rows = lax.dynamic_slice_in_dim(solution_all, row_start, row_width, 2)
    return (forward_rows, solution_rows, far_update)


def solution(mesh):
    in_specs = (
        P(None, None, "row", None),
        P(),
        P(None, None, None, "row", "col"),
        P(),
        P(None, None, "row", "col"),
        P(None, None, "row"),
        P(),
        P(None, "col", "row"),
        P(("row", "col"), None),
        P("row", None),
    )
    out_specs = (P(None, None, "row", None), P(None, None, "row", None), P(("row", "col"), None))
    return jax.shard_map(
        on_device, mesh=mesh, in_specs=in_specs, out_specs=out_specs, check_vma=False
    )
```

profile of v0, /device:TPU:0, one launch (start us, length us, event | category | flops | bytes accessed | tf_op | source)
XLA Modules:
  0.0 859.8 jit_solution(2775651494124286492)
XLA Ops:
  7.2 3.1 gather_fusion
  12.3 25.3 %all-gather.6.cloned.1.call-done = f32[3,6,512,64]{2,3,0,1:T(8,128)} async-done(((f32[3,6,128,64]{2,3,0,1:T(8,128)}), f32[3,6,512,64]{2,3,0,1:T(8,128)}) %all-gather.6.cloned.1.call-update) | async-done | bytes 2359312 | tf_op jit(solution)/shard_map/all_gather | solution.py:82
  37.6 3.3 copy.100
  41.8 14.5 %fusion.66 = f32[1,4,64,64]{2,3,1,0:T(8,128)S(1)} fusion(f32[4,64,8192]{2,1,0:T(8,128)} %param.19, f32[8192,64]{0,1:T(8,128)S(1)} %copy-done), kind=kOutput, calls=%fused_computation.86 | convolution fusion | flops 1610612736 | bytes 10551296 | tf_op jit(solution)/shard_map/pjr,rk->pjk/dot_general | solution.py:113
  59.6 3.7 fusion.14
  63.3 360.3 %all-gather.8.cloned.1.call-done = f32[3,6,512,512]{2,3,1,0:T(8,128)} async-done(((f32[3,6,512,64]{2,3,1,0:T(8,128)}), f32[3,6,512,512]{2,3,1,0:T(8,128)}) %all-gather.8.cloned.1.call-update) | async-done | bytes 18874384 | tf_op jit(solution)/shard_map/all_gather | solution.py:83
  423.6 3.1 fusion.59
  426.7 3.7 fusion.10
  436.5 3.7 fusion.6
  446.3 3.3 fusion.39
  449.6 3.7 fusion.2
  454.0 6.3 scatter_custom_fusion
  462.1 129.6 %all-reduce.6.cloned.1.call-done = (f32[1,4,512,64]{2,3,1,0:T(8,128)}, f32[1,4,512,64]{2,3,1,0:T(8,128)}) async-done(((f32[1,4,512,64]{2,3,1,0:T(8,128)}, f32[1,4,512,64]{2,3,1,0:T(8,128)}), (f32[1,4,512,64]{2,3,1,0:T(8,128)}, f32[1,4,512,64]{2,3,1,0:T(8,128)})) %all-reduce.6.cloned.1.call-update) | async-done | bytes 1048592 | tf_op jit(solution)/shard_map/psum | solution.py:97
  632.3 3.5 convolution_multiply_fusion.1
  651.3 8.9 %convolution_bitcast_fusion = f32[8192,64]{0,1:T(8,128)} fusion(f32[4,64,8192]{2,1,0:T(8,128)} %param.19, f32[1,4,512,64]{2,3,1,0:T(8,128)S(1)} %get-tuple-element.26, s32[]{:T(128)S(6)} %select_n.32), kind=kOutput, calls=%fused_computation.3 | convolution fusion | flops 1610612736 | bytes 10616836 | tf_op jit(solution)/shard_map/pjr,pjk->rk/dot_general | solution.py:108
  660.3 120.1 %all-reduce.4.cloned.1.call-done = f32[2,4,512,64]{2,3,0,1:T(8,128)} async-done(((f32[2,4,512,64]{2,3,0,1:T(8,128)}), f32[2,4,512,64]{2,3,0,1:T(8,128)}) %all-reduce.4.cloned.1.call-update) | async-done | bytes 1048592 | tf_op jit(solution)/shard_map/psum | solution.py:126
  783.5 3.8 fusion.41
  787.4 3.1 fusion.4
  790.5 3.8 fusion.53
  794.3 3.8 fusion.45
  801.1 3.8 fusion.61
  804.9 3.8 fusion.57
  808.7 3.8 fusion.49
  817.1 33.9 %reduce-scatter.2.cloned.1.call-done = f32[1024,64]{0,1:T(8,128)} async-done(((f32[8192,64]{0,1:T(8,128)}), f32[1024,64]{0,1:T(8,128)}) %reduce-scatter.2.cloned.1.call-update) | async-done | bytes 262160 | tf_op jit(solution)/shard_map/reduce_scatter | solution.py:107
  (105 shorter events, 89.2 us)
Async XLA Ops:
  7.2 34.6 %copy-start = (f32[8192,64]{0,1:T(8,128)S(1)}, f32[8192,64]{0,1:T(8,128)}, u32[]{:S(2)}) copy-start(f32[8192,64]{0,1:T(8,128)} %param.21) | copy-start | bytes 6291460
  7.2 49.8 %copy-start.10 = (s32[3,4,4]{2,1,0:T(4,128)S(1)}, s32[3,4,4]{2,1,0:T(4,128)}, u32[]{:S(2)}) copy-start(s32[3,4,4]{2,1,0:T(4,128)} %param.15) | copy-start | bytes 580
  7.2 50.0 %copy-start.9 = (s32[2,4,128]{2,1,0:T(4,128)S(1)}, s32[2,4,128]{2,1,0:T(4,128)}, u32[]{:S(2)}) copy-start(s32[2,4,128]{2,1,0:T(4,128)} %param.17) | copy-start | bytes 12292
  7.2 30.4 %all-gather.6.cloned.1.call-start = ((), (), s32[]{:S(2)}) async-start(), calls=%async_computation.2 | async-start | bytes 2949120 | tf_op jit(solution)/shard_map/all_gather | solution.py:82
  10.4 49.2 %all-gather.4.cloned.1.call-start = ((), (), s32[]{:S(2)}) async-start(), calls=%async_computation.1 | async-start | bytes 1966080 | tf_op jit(solution)/shard_map/all_gather | solution.py:84
  12.2 411.4 %all-gather.8.cloned.1.call-start = ((), (), s32[]{:S(2)}) async-start(), calls=%async_computation.3 | async-start | bytes 21233664 | tf_op jit(solution)/shard_map/all_gather | solution.py:83
  40.9 550.8 %all-reduce.6.cloned.1.call-start = ((), (), s32[]{:S(2)}) async-start(), calls=%async_computation.6 | async-start | bytes 2097152 | tf_op jit(solution)/shard_map/psum | solution.py:97
  57.0 392.6 %copy-start.5 = (f32[1,4,512,64]{2,3,1,0:T(8,128)}, f32[1,4,512,64]{2,3,1,0:T(8,128)S(1)}, u32[]{:S(2)}) copy-start(f32[1,4,512,64]{2,3,1,0:T(8,128)S(1)} %dynamic_update_slice.8) | copy-start | bytes 1572868
  57.2 392.4 %copy-start.11 = (f32[2]{0:T(128)}, f32[2]{0:T(128)S(1)}, u32[]{:S(2)}) copy-start(f32[2]{0:T(128)S(1)} %get-tuple-element.19) | copy-start | bytes 28
  57.2 392.4 %copy-start.13 = (f32[2]{0:T(128)}, f32[2]{0:T(128)S(1)}, u32[]{:S(2)}) copy-start(f32[2]{0:T(128)S(1)} %get-tuple-element.23) | copy-start | bytes 28
  57.2 392.4 %copy-start.15 = (f32[2]{0:T(128)}, f32[2]{0:T(128)S(1)}, u32[]{:S(2)}) copy-start(f32[2]{0:T(128)S(1)} %get-tuple-element.21) | copy-start | bytes 28
  57.2 392.4 %copy-start.17 = (f32[2]{0:T(128)}, f32[2]{0:T(128)S(1)}, u32[]{:S(2)}) copy-start(f32[2]{0:T(128)S(1)} %get-tuple-element.18) | copy-start | bytes 28
  423.6 29.7 %copy-start.6 = (f32[2,4,128,64]{2,3,1,0:T(8,128)S(1)}, f32[2,4,128,64]{2,3,1,0:T(8,128)}, u32[]{:S(2)}) copy-start(f32[2,4,128,64]{2,3,1,0:T(8,128)} %param.16) | copy-start | bytes 786436
  461.4 319.0 %all-reduce.4.cloned.1.call-start = ((), (), s32[]{:S(2)}) async-start(), calls=%async_computation.4 | async-start | bytes 2097152 | tf_op jit(solution)/shard_map/psum | solution.py:126
  591.7 25.7 %copy-start.7 = (f32[1,4,512,64]{2,3,1,0:T(8,128)S(1)}, f32[1,4,512,64]{2,3,1,0:T(8,128)}, u32[]{:S(2)}) copy-start(f32[1,4,512,64]{2,3,1,0:T(8,128)} %get-tuple-element.25) | copy-start | bytes 1572868
  645.0 138.5 %copy-start.18 = (f32[2]{0:T(128)S(1)}, f32[2]{0:T(128)}, u32[]{:S(2)}) copy-start(f32[2]{0:T(128)} %copy-done.17) | copy-start | bytes 28
  648.6 142.0 %copy-start.16 = (f32[2]{0:T(128)S(1)}, f32[2]{0:T(128)}, u32[]{:S(2)}) copy-start(f32[2]{0:T(128)} %copy-done.15) | copy-start | bytes 28
  650.3 200.7 %reduce-scatter.2.cloned.1.call-start = ((), (), s32[]{:S(2)}) async-start(), calls=%async_computation.5 | async-start | bytes 2359296 | tf_op jit(solution)/shard_map/reduce_scatter | solution.py:107
  651.3 143.0 %copy-start.12 = (f32[2]{0:T(128)S(1)}, f32[2]{0:T(128)}, u32[]{:S(2)}) copy-start(f32[2]{0:T(128)} %copy-done.11) | copy-start | bytes 28
  651.3 149.8 %copy-start.14 = (f32[2]{0:T(128)S(1)}, f32[2]{0:T(128)}, u32[]{:S(2)}) copy-start(f32[2]{0:T(128)} %copy-done.13) | copy-start | bytes 28
  783.5 31.9 %copy-start.3 = (f32[1,4,512,64]{2,3,0,1:T(8,128)S(1)}, f32[1,4,512,64]{2,3,0,1:T(8,128)}, u32[]{:S(2)}) copy-start(f32[1,4,512,64]{2,3,0,1:T(8,128)} %get-tuple-element.28) | copy-start | bytes 1572868
  783.5 31.9 %copy-start.4 = (f32[1,4,512,64]{2,3,0,1:T(8,128)S(1)}, f32[1,4,512,64]{2,3,0,1:T(8,128)}, u32[]{:S(2)}) copy-start(f32[1,4,512,64]{2,3,0,1:T(8,128)} %get-tuple-element.27) | copy-start | bytes 1572868
  787.4 65.4 %copy-start.1 = (f32[8192,64]{0,1:T(8,128)S(1)}, f32[8192,64]{0,1:T(8,128)}, u32[]{:S(2)}) copy-start(f32[8192,64]{0,1:T(8,128)} %param.21) | copy-start | bytes 6291460
  790.5 60.5 %copy-start.8 = (f32[1024,64]{0,1:T(8,128)S(1)}, f32[1024,64]{0,1:T(8,128)}, u32[]{:S(2)}) copy-start(f32[1024,64]{0,1:T(8,128)} %param.20) | copy-start | bytes 786436
  (1 other events, 1.0 us)
Sparse Core Ops, SparseCore 0:
  10.5 27.0 all-gather.5
  39.7 19.8 all-gather.3
  61.1 362.4 all-gather.7
  461.5 130.1 all-reduce.5
  650.4 129.9 all-reduce.3
  783.8 67.1 reduce-scatter.1
where the time goes:
time: 866 us; the launch traced here: 860 us
  waiting for transfers between devices  672 us (78%)
  matrix products  145 us (17%)
  local copies, waits for them, and re-layouts  17.7 us (2%)
  between operations  14.7 us (2%)
  other arithmetic  10.7 us (1%)
    all_gather x1, waiting for transfers between devices, on_device(): lower_blocks = lax.all_gather(lower_part, 'col', axis=3, tiled=True)  360 us
    psum x1, waiting for transfers between devices, on_device(): ancestor = lax.psum(spread, ('row', 'col')).reshape(panels, width, columns)  130 us
    psum x1, waiting for transfers between devices, on_device(): lax.psum(place_columns(child_extra, col_start, width), ('row', 'col'))  120 us
    dot_general x12, matrix products, whole_backward(): jnp.einsum('bij,bik->bjk', block, solved[later], precision=FULL_PRECISION)  41.1 us
    dot_general x12, matrix products, whole_forward(): jnp.einsum('bij,bjk->bik', block, solved[earlier], precision=FULL_PRECISION)  34.6 us
    reduce_scatter x1, waiting for transfers between devices, on_device(): lax.psum_scatter(jnp.einsum('pjr,pjk->rk', far_factor, parent_cols, preci...  33.9 us
    all_gather x1, waiting for transfers between devices, on_device(): lower_part = lax.all_gather(lower_local, 'row', axis=2, tiled=True)  25.3 us
    dot_general x8, matrix products, whole_forward(): jnp.einsum('bij,bjk->bik', inverse[:, panel_index], residual, precision=F...  24.4 us
  transfers between devices with their start and end apart: 6, of which 6 were waited for; matrix products, arithmetic and copies ran while one was open for 8% of the time, Pallas kernels for 0%

commit v1 on v0

--- a/solution.py
+++ b/solution.py
@@ -123,7 +123,9 @@
     parent_flat = parent_solution[0].reshape(panels * width, columns)
     picked = parent_flat[anc_rows] * live_rows[..., None]
     child_extra = jnp.einsum("spaj,spak->spjk", anc_values, picked, precision=FULL_PRECISION)
-    extra_whole = lax.psum(place_columns(child_extra, col_start, width), ("row", "col"))
+    block_2 = place_columns(child_extra, col_start, width)
+    pieces = lax.all_gather(block_2, ("row", "col"))
+    extra_whole = jnp.sum(pieces, axis=0)
     child_solution = whole_backward(
         child_forward, diag_inverse[:2], lower_blocks[:2], kept_blocks[:2], extra_whole, pair_of
     )

time: 866 us -> 954 us (1.10)
  waiting for transfers between devices: 672 us -> 748 us
  other arithmetic: 10.7 us -> 22.5 us
    all_gather x0 -> x1, waiting for transfers between devices: none -> 195 us  [on_device(): pieces = lax.all_gather(block_2, ('row', 'col'))]
    psum x1 -> x0, waiting for transfers between devices: 120 us -> none  [on_device(): lax.psum(place_columns(child_extra, col_start, width), ('row', 'col'))]
    reduce_sum x0 -> x1, other arithmetic: none -> 12.5 us  [on_device(): extra_whole = jnp.sum(pieces, axis=0)]
  transfers between devices with their start and end apart: 6 -> 6, of which waited for: 6 -> 6; matrix products, arithmetic and copies ran while one was open for 8% -> 6% of each run, Pallas kernels for 0% -> 0%
where the time goes in v1:
time: 954 us; the launch traced here: 948 us
  waiting for transfers between devices  748 us (78%)
  matrix products  145 us (15%)
  other arithmetic  22.5 us (2%)
  local copies, waits for them, and re-layouts  17.7 us (2%)
  between operations  14.7 us (2%)
    all_gather x1, waiting for transfers between devices, on_device(): lower_blocks = lax.all_gather(lower_part, 'col', axis=3, tiled=True)  360 us
    all_gather x1, waiting for transfers between devices, on_device(): pieces = lax.all_gather(block_2, ('row', 'col'))  195 us
    psum x1, waiting for transfers between devices, on_device(): ancestor = lax.psum(spread, ('row', 'col')).reshape(panels, width, columns)  130 us
    dot_general x12, matrix products, whole_backward(): jnp.einsum('bij,bik->bjk', block, solved[later], precision=FULL_PRECISION)  40.7 us
    dot_general x12, matrix products, whole_forward(): jnp.einsum('bij,bjk->bik', block, solved[earlier], precision=FULL_PRECISION)  34.8 us
    reduce_scatter x1, waiting for transfers between devices, on_device(): lax.psum_scatter(jnp.einsum('pjr,pjk->rk', far_factor, parent_cols, preci...  34.5 us
    all_gather x1, waiting for transfers between devices, on_device(): lower_part = lax.all_gather(lower_local, 'row', axis=2, tiled=True)  25.3 us
    dot_general x8, matrix products, whole_forward(): jnp.einsum('bij,bjk->bik', inverse[:, panel_index], residual, precision=F...  24.4 us
  transfers between devices with their start and end apart: 6, of which 6 were waited for; matrix products, arithmetic and copies ran while one was open for 6% of the time, Pallas kernels for 0%

profile of v1, /device:TPU:0, one launch (start us, length us, event | category | flops | bytes accessed | tf_op | source)
XLA Modules:
  0.0 948.3 jit_solution(2089855624483810125)
XLA Ops:
  7.3 3.1 gather_fusion
  12.3 25.3 %all-gather.7.cloned.1.call-done = f32[3,6,512,64]{2,3,0,1:T(8,128)} async-done(((f32[3,6,128,64]{2,3,0,1:T(8,128)}), f32[3,6,512,64]{2,3,0,1:T(8,128)}) %all-gather.7.cloned.1.call-update) | async-done | bytes 2359312 | tf_op jit(solution)/shard_map/all_gather | solution.py:82
  37.6 3.4 copy.94
  41.0 14.5 %fusion.66 = f32[1,4,64,64]{2,3,1,0:T(8,128)S(1)} fusion(f32[4,64,8192]{2,1,0:T(8,128)} %param.19, f32[8192,64]{0,1:T(8,128)S(1)} %copy-done), kind=kOutput, calls=%fused_computation.86 | convolution fusion | flops 1610612736 | bytes 10551296 | tf_op jit(solution)/shard_map/pjr,rk->pjk/dot_general | solution.py:113
  59.6 3.7 fusion.14
  63.3 360.3 %all-gather.9.cloned.1.call-done = f32[3,6,512,512]{2,3,1,0:T(8,128)} async-done(((f32[3,6,512,64]{2,3,1,0:T(8,128)}), f32[3,6,512,512]{2,3,1,0:T(8,128)}) %all-gather.9.cloned.1.call-update) | async-done | bytes 18874384 | tf_op jit(solution)/shard_map/all_gather | solution.py:83
  426.7 3.7 fusion.10
  436.5 3.7 fusion.6
  446.3 3.2 fusion.39
  449.6 3.7 fusion.2
  454.0 6.3 scatter_custom_fusion
  462.1 129.5 %all-reduce.3.cloned.1.call-done = (f32[1,4,512,64]{2,3,1,0:T(8,128)}, f32[1,4,512,64]{2,3,1,0:T(8,128)}) async-done(((f32[1,4,512,64]{2,3,1,0:T(8,128)}, f32[1,4,512,64]{2,3,1,0:T(8,128)}), (f32[1,4,512,64]{2,3,1,0:T(8,128)}, f32[1,4,512,64]{2,3,1,0:T(8,128)})) %all-reduce.3.cloned.1.call-update) | async-done | bytes 1048592 | tf_op jit(solution)/shard_map/psum | solution.py:97
  618.4 9.2 convolution_bitcast_fusion
  660.3 34.5 %reduce-scatter.2.cloned.1.call-done = f32[1024,64]{0,1:T(8,128)} async-done(((f32[8192,64]{0,1:T(8,128)}), f32[1024,64]{0,1:T(8,128)}) %reduce-scatter.2.cloned.1.call-update) | async-done | bytes 262160 | tf_op jit(solution)/shard_map/reduce_scatter | solution.py:107
  696.5 195.5 %all-gather.11.cloned.1.call-done = f32[32,2,4,512,64]{3,4,2,1,0:T(8,128)} async-done(((f32[1,2,4,512,64]{3,4,2,1,0:T(8,128)}), f32[32,2,4,512,64]{3,4,2,1,0:T(8,128)}) %all-gather.11.cloned.1.call-update) | async-done | bytes 33554448 | tf_op jit(solution)/shard_map/all_gather | solution.py:127
  892.0 12.5 %reduce_sum.9 = f32[2,4,512,64]{2,3,1,0:T(8,128)S(1)} reduce(f32[32,2,4,512,64]{3,4,2,1,0:T(8,128)} %all-gather.11.cloned.1.call-done, f32[]{:T(128)} %constant.13.clone.1), dimensions={0}, to_apply=%region_3.0 | reduce | flops 8126464 | bytes 34603012 | tf_op jit(solution)/shard_map/reduce_sum | solution.py:128
  904.5 3.4 fusion
  907.9 3.8 fusion.41
  911.7 3.1 fusion.4
  914.9 3.8 fusion.53
  918.6 3.7 fusion.45
  925.4 3.8 fusion.61
  929.1 3.7 fusion.57
  932.9 3.7 fusion.49
  (91 shorter events, 92.5 us)
Async XLA Ops:
  7.2 33.9 %copy-start = (f32[8192,64]{0,1:T(8,128)S(1)}, f32[8192,64]{0,1:T(8,128)}, u32[]{:S(2)}) copy-start(f32[8192,64]{0,1:T(8,128)} %param.21) | copy-start | bytes 6291460
  7.2 49.1 %copy-start.10 = (s32[3,4,4]{2,1,0:T(4,128)S(1)}, s32[3,4,4]{2,1,0:T(4,128)}, u32[]{:S(2)}) copy-start(s32[3,4,4]{2,1,0:T(4,128)} %param.15) | copy-start | bytes 580
  7.2 49.3 %copy-start.11 = (s32[2,4]{1,0:T(2,128)S(1)}, s32[2,4]{1,0:T(2,128)}, u32[]{:S(2)}) copy-start(s32[2,4]{1,0:T(2,128)} %param.18) | copy-start | bytes 100
  7.2 49.4 %copy-start.9 = (s32[2,4,128]{2,1,0:T(4,128)S(1)}, s32[2,4,128]{2,1,0:T(4,128)}, u32[]{:S(2)}) copy-start(s32[2,4,128]{2,1,0:T(4,128)} %param.17) | copy-start | bytes 12292
  7.2 30.4 %all-gather.7.cloned.1.call-start = ((), (), s32[]{:S(2)}) async-start(), calls=%async_computation.2 | async-start | bytes 2949120 | tf_op jit(solution)/shard_map/all_gather | solution.py:82
  10.4 49.2 %all-gather.5.cloned.1.call-start = ((), (), s32[]{:S(2)}) async-start(), calls=%async_computation.1 | async-start | bytes 1966080 | tf_op jit(solution)/shard_map/all_gather | solution.py:84
  12.2 411.4 %all-gather.9.cloned.1.call-start = ((), (), s32[]{:S(2)}) async-start(), calls=%async_computation.3 | async-start | bytes 21233664 | tf_op jit(solution)/shard_map/all_gather | solution.py:83
  41.0 550.7 %all-reduce.3.cloned.1.call-start = ((), (), s32[]{:S(2)}) async-start(), calls=%async_computation.6 | async-start | bytes 2097152 | tf_op jit(solution)/shard_map/psum | solution.py:97
  56.3 393.3 %copy-start.6 = (f32[1,4,512,64]{2,3,1,0:T(8,128)}, f32[1,4,512,64]{2,3,1,0:T(8,128)S(1)}, u32[]{:S(2)}) copy-start(f32[1,4,512,64]{2,3,1,0:T(8,128)S(1)} %dynamic_update_slice.9) | copy-start | bytes 1572868
  423.6 29.7 %copy-start.7 = (f32[2,4,128,64]{2,3,1,0:T(8,128)S(1)}, f32[2,4,128,64]{2,3,1,0:T(8,128)}, u32[]{:S(2)}) copy-start(f32[2,4,128,64]{2,3,1,0:T(8,128)} %param.16) | copy-start | bytes 786436
  461.4 233.4 %reduce-scatter.2.cloned.1.call-start = ((), (), s32[]{:S(2)}) async-start(), calls=%async_computation.5 | async-start | bytes 2359296 | tf_op jit(solution)/shard_map/reduce_scatter | solution.py:107
  596.9 30.9 %copy-start.8 = (f32[1,4,512,64]{2,3,1,0:T(8,128)S(1)}, f32[1,4,512,64]{2,3,1,0:T(8,128)}, u32[]{:S(2)}) copy-start(f32[1,4,512,64]{2,3,1,0:T(8,128)} %get-tuple-element.25) | copy-start | bytes 1572868
  627.6 264.4 %all-gather.11.cloned.1.call-start = ((), (), s32[]{:S(2)}) async-start(), calls=%async_computation.4 | async-start | bytes 34603008 | tf_op jit(solution)/shard_map/all_gather | solution.py:127
  659.3 1.0 copy-start.2
  904.5 3.4 copy-start.3
  907.9 31.7 %copy-start.4 = (f32[1,4,512,64]{2,3,0,1:T(8,128)S(1)}, f32[1,4,512,64]{2,3,0,1:T(8,128)}, u32[]{:S(2)}) copy-start(f32[1,4,512,64]{2,3,0,1:T(8,128)} %get-tuple-element.27) | copy-start | bytes 1572868
  907.9 31.7 %copy-start.5 = (f32[1,4,512,64]{2,3,0,1:T(8,128)S(1)}, f32[1,4,512,64]{2,3,0,1:T(8,128)}, u32[]{:S(2)}) copy-start(f32[1,4,512,64]{2,3,0,1:T(8,128)} %get-tuple-element.28) | copy-start | bytes 1572868
  911.7 29.6 %copy-start.1 = (f32[8192,64]{0,1:T(8,128)S(1)}, f32[8192,64]{0,1:T(8,128)}, u32[]{:S(2)}) copy-start(f32[8192,64]{0,1:T(8,128)} %param.21) | copy-start | bytes 6291460
Sparse Core Ops, SparseCore 0:
  10.5 27.0 all-gather.6
  39.7 19.8 all-gather.4
  61.1 362.4 all-gather.8
  461.5 130.0 all-reduce.2
  627.8 66.9 reduce-scatter.1
  698.0 193.9 all-gather.10
